TPU v7x, 32 devices: a whole 2x2x4 slice. The times are simulated.
32 devices in a mesh: grp: 4 (over x, core), blk: 8 (over z, y).
Axes of the slice: x: 2, y: 2, z: 4, core: 2. Of those that a mesh axis runs over, the one named last changes fastest.
Arguments:
- fine_coef: float32 [128, 20, 32, 128], P(('grp', 'blk')), may hold values from -6 to 6
- src_fine: int32 [256], P(('grp', 'blk')), may hold values from 0 to 3
- target_group: int32 [256], P(('grp', 'blk')), may hold values from 0 to 4, as said below
- slot: int32 [256], P(('grp', 'blk')), may hold values from 0 to 15
- valence_intersection: float32 [512, 20, 20], P(('grp', 'blk')), may hold values from -0.5 to 0.5
- conduction_intersection: float32 [512, 32, 32], P(('grp', 'blk')), may hold values from -1 to 1
- kernel: float32 [32, 4, 640, 640], P(('grp', 'blk')), may hold values from -0.125 to 0.125
- energies: float32 [32, 640], P(('grp', 'blk')), may hold values from 0.5 to 2
Outputs:
- applied: float32 [32, 640, 128], P(('grp', 'blk'))
Inputs may be any that keep to these rules, and one draw needn't show every extreme that they name: `src_fine`: an index among the 4 fine momenta of the device that holds the entry. `slot`: an index among the 16 intersection slots of the device that holds the entry. `target_group`: the value 4 marks an unused entry; in each device's 8 entries the used ones come first, at least 2 of them, and some device uses all.
All inputs are finite; a program needn't handle non-finite values.
Results may differ from a plain program's by a relative error of at most 0.0003.
Values sent between devices are 32-bit elements; how exact they have to be, the bound alone decides.
No kernel may reach another device: no remote copies, remote signals or barrier semaphores. Data moves between devices by JAX's collectives and lax.ppermute only.
A program may use at most 64 MiB of HBM per device.

v0:
```python
import functools

import jax
import jax.numpy as jnp
from jax import lax
from jax.experimental import pallas as pl
from jax.experimental.pallas import tpu as pltpu
from jax.sharding import PartitionSpec as P


F32, BF16 = jnp.float32, jnp.bfloat16
LANES = 128
CHUNKS = 3


def moved(value, axis, target_of):
    count = lax.axis_size(axis)
    return lax.ppermute(value, axis, [(source, target_of(source)) for source in range(count)])


def kept(array):
    return pltpu.with_memory_space_constraint(array, pltpu.HBM)


def split(value):
    high = value.astype(BF16)
    low = (value - high.astype(F32)).astype(BF16)
    return high, low


def dot_first(left, right):
    return lax.dot_general(left, right, (((0,), (0,)), ((), ())), preferred_element_type=F32)


def rotate_kernel(
    sizes, cuts, group, *rest
):
    groups, order, entries, fine, slots, val, cond, vec = sizes
    given, outs, rest = rest[:6], rest[6 : 6 + 2 * len(cuts)], rest[6 + 2 * len(cuts) :]
    held, (stage, fine_rows, turned, total, sems) = rest[:6], rest[6:]
    copies = [pltpu.make_async_copy(a, b, sems.at[i]) for i, (a, b) in enumerate(zip(given, held))]
    for copy in copies:
        copy.start()
    src, target, slot, x_ref, val_ref, cond_ref = held
    total[...] = jnp.zeros_like(total)
    for copy in copies:
        copy.wait()
    pad = stage.shape[0]
    block = val * cond
    stage[...] = jnp.zeros_like(stage)
    for f in range(fine):
        for c in range(cond):
            stage[0:val, c * vec : (c + 1) * vec] = x_ref[pl.ds(f * block + c, val, stride=cond), :]
        high, low = split(stage[...])
        fine_rows[f, 0:pad] = high
        fine_rows[f, pad : 2 * pad] = high
        fine_rows[f, 2 * pad : 3 * pad] = low

    def add_entry(e, carry):
        aim = target[e]

        @pl.when(aim < groups)
        def _():
            place = order(aim, group[0])
            which = slot[e]
            weights = val_ref[pl.ds(which, val, stride=slots), :]
            weights = jnp.concatenate([weights, jnp.zeros((pad - val, val), F32)], axis=0)
            high, low = split(weights)
            left = jnp.concatenate([high, low, high], axis=0)
            first = dot_first(left, fine_rows[src[e]])
            for c in range(cond):
                turned[pl.ds(c, val, stride=cond), :] = first[:, c * vec : (c + 1) * vec]
            wide = jnp.concatenate(
                [turned[w * cond : (w + 1) * cond, :] for w in range(val)], axis=1
            )
            high, low = split(wide)
            right = jnp.concatenate([high, high, low], axis=0)
            high, low = split(cond_ref[which])
            left = jnp.concatenate([high, low, high], axis=0)
            second = dot_first(left, right)
            for w in range(val):
                total[place, w * cond : (w + 1) * cond, :] += second[:, w * vec : (w + 1) * vec]

        return carry

    lax.fori_loop(0, entries, add_entry, 0)
    half = groups // 2
    for i, (start, width) in enumerate(cuts):
        outs[2 * i][...] = total[0:half, start : start + width, :]
        outs[2 * i + 1][...] = total[half:groups, start : start + width, :]


def apply_kernel(start, width, offsets, has_total, kernel_hbm, *rest):
    rest = list(rest)
    energies = rest.pop(0) if 0 in offsets else None
    total = rest.pop(0) if has_total else None
    values = [rest.pop(0) for _ in offsets]
    out, blocks, levels, sems = rest
    copies = []
    if energies is not None:
        fetched = pltpu.make_async_copy(
            energies.at[:, pl.ds(start, width)], levels, sems.at[len(offsets)]
        )
        fetched.start()
    for i, offset in enumerate(offsets):
        copy = pltpu.make_async_copy(
            kernel_hbm.at[0, offset, :, pl.ds(start, width)], blocks.at[i], sems.at[i]
        )
        copy.start()
        copies.append(copy)
    if has_total:
        out[...] = total[...]
    else:
        out[...] = jnp.zeros_like(out)
    for i, offset in enumerate(offsets):
        value = values[i][...]
        if offset == 0:
            fetched.wait()
            for r in range(0, width, LANES):
                row = jnp.broadcast_to(
                    levels[0:1, r : r + LANES], (LANES, LANES)
                )
                out[start + r : start + r + LANES, :] += row.T * value[r : r + LANES, :]
        high, low = split(value)
        copies[i].wait()
        block_high, block_low = split(blocks[i])
        both = jnp.dot(
            block_high, jnp.concatenate([high, low], axis=1), preferred_element_type=F32
        )
        more = jnp.dot(block_low, high, preferred_element_type=F32)
        vec = value.shape[1]
        out[...] += both[:, :vec] + both[:, vec:] + more


def reversed_bits(value, bits):
    result = value * 0
    for k in range(bits):
        result = result + (((value >> k) & 1) << (bits - 1 - k))
    return result


def on_device(cuts_of, fine_coef, src, target, slot, valence, conduction, kernel, energies):
    groups = lax.axis_size("grp")
    fine, val, cond, vec = fine_coef.shape
    entries, slots = src.shape[0], valence.shape[0]
    bits = groups.bit_length() - 1
    cuts = cuts_of(val, cond)
    pairs = val * cond

    def order(aim, mine):
        return reversed_bits(aim ^ mine, bits)

    sizes = (groups, order, entries, fine, slots, val, cond, vec)
    pad = -(-val // 16) * 16
    vmem = pl.BlockSpec(memory_space=pltpu.VMEM)
    smem = pl.BlockSpec(memory_space=pltpu.SMEM)
    hbm = pl.BlockSpec(memory_space=pltpu.HBM)
    parts = pl.pallas_call(
        functools.partial(rotate_kernel, sizes, cuts),
        name="rotate",
        out_shape=[
            jax.ShapeDtypeStruct((groups // 2, width, vec), F32) for _, width in cuts for _ in range(2)
        ],
        in_specs=[smem] + [hbm] * 6,
        out_specs=[vmem] * (2 * len(cuts)),
        scratch_shapes=[
            pltpu.SMEM((entries,), jnp.int32),
            pltpu.SMEM((entries,), jnp.int32),
            pltpu.SMEM((entries,), jnp.int32),
            pltpu.VMEM((fine * pairs, vec), F32),
            pltpu.VMEM((val * slots, val), F32),
            pltpu.VMEM((slots, cond, cond), F32),
            pltpu.VMEM((pad, cond * vec), F32),
            pltpu.VMEM((fine, 3 * pad, cond * vec), BF16),
            pltpu.VMEM((pairs, vec), F32),
            pltpu.VMEM((groups, pairs, vec), F32),
            pltpu.SemaphoreType.DMA((6,)),
        ],
        compiler_params=pltpu.CompilerParams(vmem_limit_bytes=32 << 20),
    )(
        lax.axis_index("grp").astype(jnp.int32).reshape(1),
        kept(src),
        kept(target),
        kept(slot),
        kept(fine_coef.reshape(fine * pairs, vec)),
        kept(jnp.transpose(valence, (1, 0, 2)).reshape(val * slots, val)),
        kept(conduction),
    )

    owned = []
    for i in range(len(cuts)):
        keep, give = parts[2 * i], parts[2 * i + 1]
        for bit in range(bits):
            keep = keep + moved(give, "grp", lambda source: source ^ (1 << bit))
            half = keep.shape[0] // 2
            if half > 0:
                keep, give = keep[:half], keep[half:]
        owned.append(keep[0])
    result = None
    for (start, width), own in zip(cuts, owned):
        behind = shifted_back(own, kernel.shape[1])
        result = apply_part(result, kernel, energies, start, width, [0], [own])
        early = [s for s in behind if s < 3]
        late = [s for s in behind if s >= 3]
        for chosen in (early, late):
            if chosen:
                values = [behind[s] for s in chosen]
                result = apply_part(result, kernel, energies, start, width, chosen, values)
    return result[None]


def shifted_back(own, stops):
    count = lax.axis_size("blk")
    behind = {0: own}
    if count % 2 == 0 and stops > 2:
        odd = lax.axis_index("blk") % 2 == 1
        behind[2] = moved(own, "blk", lambda source: (source + 2) % count)
        mixed = jnp.where(odd, behind[2], own)
        behind[1] = moved(mixed, "blk", lambda source: source ^ 1)
    elif stops > 1:
        behind[1] = moved(own, "blk", lambda source: (source + 1) % count)
    for s in range(2, stops):
        if s not in behind:
            behind[s] = moved(behind[s - 2], "blk", lambda source: (source + 2) % count)
    del behind[0]
    return behind


def apply_part(total, kernel, energies, start, width, offsets, values):
    rows, vec = kernel.shape[2], values[0].shape[1]
    vmem = pl.BlockSpec(memory_space=pltpu.VMEM)
    operands = [kept(kernel)]
    specs = [pl.BlockSpec(memory_space=pltpu.HBM)]
    if 0 in offsets:
        operands.append(kept(energies))
        specs.append(specs[0])
    if total is not None:
        operands.append(total)
        specs.append(vmem)
    operands += values
    specs += [vmem] * len(values)
    return pl.pallas_call(
        functools.partial(apply_kernel, start, width, tuple(offsets), total is not None),
        name="apply",
        out_shape=jax.ShapeDtypeStruct((rows, vec), F32),
        in_specs=specs,
        out_specs=vmem,
        scratch_shapes=[
            pltpu.VMEM((len(offsets), rows, width), F32),
            pltpu.VMEM((1, width), F32),
            pltpu.SemaphoreType.DMA((len(offsets) + 1,)),
        ],
        compiler_params=pltpu.CompilerParams(vmem_limit_bytes=24 << 20),
    )(*operands)


def cut_evenly(val, cond):
    step = next(w for w in range(1, val + 1) if val % w == 0 and (w * cond % LANES == 0 or w == val))
    steps = val // step
    counts = [steps * (k + 1) // CHUNKS - steps * k // CHUNKS for k in range(CHUNKS)]
    cuts, start = [], 0
    for count in counts:
        if count:
            cuts.append((start * step * cond, count * step * cond))
            start += count
    return cuts


def solution(mesh):
    spec = P(("grp", "blk"))

    def body(*args):
        return on_device(cut_evenly, *args)

    return jax.shard_map(
        body, mesh=mesh, in_specs=(spec,) * 8, out_specs=spec, check_vma=False
    )
```

profile of v0, /device:TPU:0, one launch (start us, length us, event | category | flops | bytes accessed | tf_op | source)
XLA Modules:
  0.0 54.4 jit_solution(15007749130214718601)
XLA Ops:
  0.0 7.3 %rotate.1 = (f32[2,128,128]{2,1,0:T(8,128)S(1)}, f32[2,128,128]{2,1,0:T(8,128)S(1)}, f32[2,256,128]{2,1,0:T(8,128)S(1)}, f32[2,256,128]{2,1,0:T(8,128)S(1)}, f32...) custom-call(s32[1]{0:T(128)} %bitcast.group, s32[8]{0:T(128)} %rest_0_.4, s32[8]{0:T(128)} %rest_1_.1, s32[8]{0:T(128)} %rest_2_.1, ...), custom_call_target="tpu_custom_call" | custom-call | tf_op jit(solution)/shard_map/rotate/pallas_call | solution.py:158
  7.9 1.2 %collective-permute-done = f32[2,128,128]{2,1,0:T(8,128)S(1)} collective-permute-done((f32[2,128,128]{2,1,0:T(8,128)S(1)}, f32[2,128,128]{2,1,0:T(8,128)S(1)}, u32[]{:S(2)}, u32[]{:S(2)}) %collective-permute-start) | collective-permute-done | bytes 131104 | tf_op jit(solution)/shard_map/ppermute | solution.py:18
  9.2 1.9 %collective-permute-start.1 = (f32[1,128,128]{2,1,0:T(8,128)S(1)}, f32[1,128,128]{2,1,0:T(8,128)S(1)}, u32[]{:S(2)}, u32[]{:S(2)}) collective-permute-start(f32[1,128,128]{2,1,0:T(8,128)S(1)} %slice.25), channel_id=1, source_target_pairs={{0,16},{8,24},{16,0},{24,8},{1,17},{9,25},{17,1},{25,9},{2,18},{10... | collective-permute-start | bytes 196616 | tf_op jit(solution)/shard_map/ppermute | solution.py:18
  11.4 2.1 %collective-permute-done.1 = f32[1,128,128]{2,1,0:T(8,128)S(1)} collective-permute-done((f32[1,128,128]{2,1,0:T(8,128)S(1)}, f32[1,128,128]{2,1,0:T(8,128)S(1)}, u32[]{:S(2)}, u32[]{:S(2)}) %collective-permute-start.1) | collective-permute-done | bytes 65568 | tf_op jit(solution)/shard_map/ppermute | solution.py:18
  13.5 0.9 %collective-permute-start.2 = (f32[128,128]{1,0:T(8,128)S(1)}, f32[128,128]{1,0:T(8,128)S(1)}, u32[]{:S(2)}, u32[]{:S(2)}) collective-permute-start(f32[128,128]{1,0:T(8,128)S(1)} %fusion.2.rest_1_), channel_id=1, source_target_pairs={{0,2},{1,3},{2,4},{3,5},{4,6},{5,7},{6,0},{7,1},{8,10},{9,11},{10,... | collective-permute-start | bytes 196616 | tf_op jit(solution)/shard_map/ppermute | solution.py:18
  14.5 2.1 %collective-permute-start.6 = (f32[1,256,128]{2,1,0:T(8,128)S(1)}, f32[1,256,128]{2,1,0:T(8,128)S(1)}, u32[]{:S(2)}, u32[]{:S(2)}) collective-permute-start(f32[1,256,128]{2,1,0:T(8,128)S(1)} %slice.27), channel_id=1, source_target_pairs={{0,16},{8,24},{16,0},{24,8},{1,17},{9,25},{17,1},{25,9},{2,18},{10... | collective-permute-start | bytes 393224 | tf_op jit(solution)/shard_map/ppermute | solution.py:18
  16.7 0.9 %collective-permute-done.11 = f32[1,256,128]{2,1,0:T(8,128)S(1)} collective-permute-done((f32[1,256,128]{2,1,0:T(8,128)S(1)}, f32[1,256,128]{2,1,0:T(8,128)S(1)}, u32[]{:S(2)}, u32[]{:S(2)}) %collective-permute-start.11) | collective-permute-done | bytes 131104 | tf_op jit(solution)/shard_map/ppermute | solution.py:18
  17.5 2.5 %collective-permute-start.12 = (f32[256,128]{1,0:T(8,128)S(1)}, f32[256,128]{1,0:T(8,128)S(1)}, u32[]{:S(2)}, u32[]{:S(2)}) collective-permute-start(f32[256,128]{1,0:T(8,128)S(1)} %fusion.rest_2_), channel_id=1, source_target_pairs={{0,2},{1,3},{2,4},{3,5},{4,6},{5,7},{6,0},{7,1},{8,10},{9,11},{10,... | collective-permute-start | bytes 393224 | tf_op jit(solution)/shard_map/ppermute | solution.py:18
  20.0 2.9 %collective-permute-start.7 = (f32[256,128]{1,0:T(8,128)S(1)}, f32[256,128]{1,0:T(8,128)S(1)}, u32[]{:S(2)}, u32[]{:S(2)}) collective-permute-start(f32[256,128]{1,0:T(8,128)S(1)} %fusion.1.rest_2_), channel_id=1, source_target_pairs={{0,2},{1,3},{2,4},{3,5},{4,6},{5,7},{6,0},{7,1},{8,10},{9,11},{10,... | collective-permute-start | bytes 393224 | tf_op jit(solution)/shard_map/ppermute | solution.py:18
  22.9 2.1 %collective-permute-done.12.rest_1_ = f32[256,128]{1,0:T(8,128)S(1)} collective-permute-done((f32[256,128]{1,0:T(8,128)S(1)}, f32[256,128]{1,0:T(8,128)S(1)}, u32[]{:S(2)}, u32[]{:S(2)}) %collective-permute-start.12) | collective-permute-done | bytes 131104 | tf_op jit(solution)/shard_map/ppermute | solution.py:18
  25.1 1.4 %collective-permute-start.13 = (f32[256,128]{1,0:T(8,128)S(1)}, f32[256,128]{1,0:T(8,128)S(1)}, u32[]{:S(2)}, u32[]{:S(2)}) collective-permute-start(f32[256,128]{1,0:T(8,128)S(1)} %broadcast_select_fusion), channel_id=1, source_target_pairs={{0,1},{1,0},{2,3},{3,2},{4,5},{5,4},{6,7},{7,6},{8,9},{9,8},{10,11... | collective-permute-start | bytes 393224 | tf_op jit(solution)/shard_map/ppermute | solution.py:18
  27.2 3.7 %collective-permute-start.8 = (f32[256,128]{1,0:T(8,128)S(1)}, f32[256,128]{1,0:T(8,128)S(1)}, u32[]{:S(2)}, u32[]{:S(2)}) collective-permute-start(f32[256,128]{1,0:T(8,128)S(1)} %broadcast_select_fusion.1), channel_id=1, source_target_pairs={{0,1},{1,0},{2,3},{3,2},{4,5},{5,4},{6,7},{7,6},{8,9},{9,8},{10,11... | collective-permute-start | bytes 393224 | tf_op jit(solution)/shard_map/ppermute | solution.py:18
  31.0 2.8 %collective-permute-done.8.rest_2_ = f32[256,128]{1,0:T(8,128)S(1)} collective-permute-done((f32[256,128]{1,0:T(8,128)S(1)}, f32[256,128]{1,0:T(8,128)S(1)}, u32[]{:S(2)}, u32[]{:S(2)}) %collective-permute-start.8) | collective-permute-done | bytes 131104 | tf_op jit(solution)/shard_map/ppermute | solution.py:18
  34.1 1.9 %collective-permute-start.14 = (f32[256,128]{1,0:T(8,128)S(1)}, f32[256,128]{1,0:T(8,128)S(1)}, u32[]{:S(2)}, u32[]{:S(2)}) collective-permute-start(f32[256,128]{1,0:T(8,128)S(1)} %collective-permute-done.13.rest_2_), channel_id=1, source_target_pairs={{0,2},{1,3},{2,4},{3,5},{4,6},{5,7},{6,0},{7,1},{8,10},{9,11},{10,... | collective-permute-start | bytes 393224 | tf_op jit(solution)/shard_map/ppermute | solution.py:18
  36.7 1.3 %apply.9.rest_0_ = f32[640,128]{1,0:T(8,128)S(1)} custom-call(f32[1,4,640,640]{3,2,1,0:T(8,128)} %kernel_hbm.17, f32[1,640]{1,0:T(1,128)} %rest_0_.7, f32[128,128]{1,0:T(8,128)S(1)} %fusion.2.rest_1_), custom_call_target="tpu_custom_call" | custom-call | tf_op jit(solution)/shard_map/apply/pallas_call | solution.py:242
  37.9 1.8 %apply.10.rest_0_ = f32[640,128]{1,0:T(8,128)S(1)} custom-call(f32[1,4,640,640]{3,2,1,0:T(8,128)} %kernel_hbm.17, f32[640,128]{1,0:T(8,128)S(1)} %apply.9.rest_0_, f32[128,128]{1,0:T(8,128)S(1)} %collective-permute-done.2.rest_1_, f32[128,128]{1,0:T(8,128)S(1)} %collective-permute-done.3.rest_2_), custom_call_target="tpu_custom_call" | custom-call | tf_op jit(solution)/shard_map/apply/pallas_call | solution.py:242
  39.7 3.1 %collective-permute-done.4.rest_1_ = f32[128,128]{1,0:T(8,128)S(1)} collective-permute-done((f32[128,128]{1,0:T(8,128)S(1)}, f32[128,128]{1,0:T(8,128)S(1)}, u32[]{:S(2)}, u32[]{:S(2)}) %collective-permute-start.4) | collective-permute-done | bytes 65568 | tf_op jit(solution)/shard_map/ppermute | solution.py:18
  42.9 1.3 %apply.11.rest_1_ = f32[640,128]{1,0:T(8,128)S(1)} custom-call(f32[1,4,640,640]{3,2,1,0:T(8,128)} %kernel_hbm.17, f32[640,128]{1,0:T(8,128)S(1)} %apply.10.rest_0_, f32[128,128]{1,0:T(8,128)S(1)} %collective-permute-done.4.rest_1_), custom_call_target="tpu_custom_call" | custom-call | tf_op jit(solution)/shard_map/apply/pallas_call | solution.py:242
  44.2 1.5 %apply.12.rest_0_ = f32[640,128]{1,0:T(8,128)S(1)} custom-call(f32[1,4,640,640]{3,2,1,0:T(8,128)} %kernel_hbm.17, f32[1,640]{1,0:T(1,128)} %rest_0_.7, f32[640,128]{1,0:T(8,128)S(1)} %apply.11.rest_1_, f32[256,128]{1,0:T(8,128)S(1)} %fusion.1.rest_2_), custom_call_target="tpu_custom_call" | custom-call | tf_op jit(solution)/shard_map/apply/pallas_call | solution.py:242
  45.6 1.8 %apply.13.rest_0_ = f32[640,128]{1,0:T(8,128)S(1)} custom-call(f32[1,4,640,640]{3,2,1,0:T(8,128)} %kernel_hbm.17, f32[640,128]{1,0:T(8,128)S(1)} %apply.12.rest_0_, f32[256,128]{1,0:T(8,128)S(1)} %collective-permute-done.7.rest_1_, f32[256,128]{1,0:T(8,128)S(1)} %collective-permute-done.8.rest_2_), custom_call_target="tpu_custom_call" | custom-call | tf_op jit(solution)/shard_map/apply/pallas_call | solution.py:242
  47.4 1.5 %apply.14.rest_1_ = f32[640,128]{1,0:T(8,128)S(1)} custom-call(f32[1,4,640,640]{3,2,1,0:T(8,128)} %kernel_hbm.17, f32[640,128]{1,0:T(8,128)S(1)} %apply.13.rest_0_, f32[256,128]{1,0:T(8,128)S(1)} %collective-permute-done.9.rest_1_), custom_call_target="tpu_custom_call" | custom-call | tf_op jit(solution)/shard_map/apply/pallas_call | solution.py:242
  48.9 1.5 %apply.15.rest_0_ = f32[640,128]{1,0:T(8,128)S(1)} custom-call(f32[1,4,640,640]{3,2,1,0:T(8,128)} %kernel_hbm.17, f32[1,640]{1,0:T(1,128)} %rest_0_.7, f32[640,128]{1,0:T(8,128)S(1)} %apply.14.rest_1_, f32[256,128]{1,0:T(8,128)S(1)} %fusion.rest_2_), custom_call_target="tpu_custom_call" | custom-call | tf_op jit(solution)/shard_map/apply/pallas_call | solution.py:242
  50.4 1.8 %apply.16.rest_0_ = f32[640,128]{1,0:T(8,128)S(1)} custom-call(f32[1,4,640,640]{3,2,1,0:T(8,128)} %kernel_hbm.17, f32[640,128]{1,0:T(8,128)S(1)} %apply.15.rest_0_, f32[256,128]{1,0:T(8,128)S(1)} %collective-permute-done.12.rest_1_, f32[256,128]{1,0:T(8,128)S(1)} %collective-permute-done.13.rest_2_), custom_call_target="tpu_custom_call" | custom-call | tf_op jit(solution)/shard_map/apply/pallas_call | solution.py:242
  52.2 2.2 %apply.17 = f32[640,128]{1,0:T(8,128)} custom-call(f32[1,4,640,640]{3,2,1,0:T(8,128)} %kernel_hbm.17, f32[640,128]{1,0:T(8,128)S(1)} %apply.16.rest_0_, f32[256,128]{1,0:T(8,128)S(1)} %collective-permute-done.14.rest_1_), custom_call_target="tpu_custom_call" | custom-call | tf_op jit(solution)/shard_map/apply/pallas_call | solution.py:242
  (28 shorter events, 2.8 us)
Async XLA Ops:
  7.3 3.7 %collective-permute-start.10 = (f32[2,256,128]{2,1,0:T(8,128)S(1)}, f32[2,256,128]{2,1,0:T(8,128)S(1)}, u32[]{:S(2)}, u32[]{:S(2)}) collective-permute-start(f32[2,256,128]{2,1,0:T(8,128)S(1)} %get-tuple-element.16), channel_id=1, source_target_pairs={{0,8},{8,0},{16,24},{24,16},{1,9},{9,1},{17,25},{25,17},{2,10},{10... | collective-permute-start | bytes 786440 | tf_op jit(solution)/shard_map/ppermute | solution.py:18
  7.4 1.7 %collective-permute-start = (f32[2,128,128]{2,1,0:T(8,128)S(1)}, f32[2,128,128]{2,1,0:T(8,128)S(1)}, u32[]{:S(2)}, u32[]{:S(2)}) collective-permute-start(f32[2,128,128]{2,1,0:T(8,128)S(1)} %get-tuple-element.12), channel_id=1, source_target_pairs={{0,8},{8,0},{16,24},{24,16},{1,9},{9,1},{17,25},{25,17},{2,10},{10... | collective-permute-start | bytes 393224 | tf_op jit(solution)/shard_map/ppermute | solution.py:18
  9.2 4.4 %collective-permute-start.1 = (f32[1,128,128]{2,1,0:T(8,128)S(1)}, f32[1,128,128]{2,1,0:T(8,128)S(1)}, u32[]{:S(2)}, u32[]{:S(2)}) collective-permute-start(f32[1,128,128]{2,1,0:T(8,128)S(1)} %slice.25), channel_id=1, source_target_pairs={{0,16},{8,24},{16,0},{24,8},{1,17},{9,25},{17,1},{25,9},{2,18},{10... | collective-permute-start | bytes 196616 | tf_op jit(solution)/shard_map/ppermute | solution.py:18
  11.0 3.4 %collective-permute-start.5 = (f32[2,256,128]{2,1,0:T(8,128)S(1)}, f32[2,256,128]{2,1,0:T(8,128)S(1)}, u32[]{:S(2)}, u32[]{:S(2)}) collective-permute-start(f32[2,256,128]{2,1,0:T(8,128)S(1)} %get-tuple-element.14), channel_id=1, source_target_pairs={{0,8},{8,0},{16,24},{24,16},{1,9},{9,1},{17,25},{25,17},{2,10},{10... | collective-permute-start | bytes 786440 | tf_op jit(solution)/shard_map/ppermute | solution.py:18
  11.1 6.4 %collective-permute-start.11 = (f32[1,256,128]{2,1,0:T(8,128)S(1)}, f32[1,256,128]{2,1,0:T(8,128)S(1)}, u32[]{:S(2)}, u32[]{:S(2)}) collective-permute-start(f32[1,256,128]{2,1,0:T(8,128)S(1)} %slice.29), channel_id=1, source_target_pairs={{0,16},{8,24},{16,0},{24,8},{1,17},{9,25},{17,1},{25,9},{2,18},{10... | collective-permute-start | bytes 393224 | tf_op jit(solution)/shard_map/ppermute | solution.py:18
  13.5 17.3 %collective-permute-start.2 = (f32[128,128]{1,0:T(8,128)S(1)}, f32[128,128]{1,0:T(8,128)S(1)}, u32[]{:S(2)}, u32[]{:S(2)}) collective-permute-start(f32[128,128]{1,0:T(8,128)S(1)} %fusion.2.rest_1_), channel_id=1, source_target_pairs={{0,2},{1,3},{2,4},{3,5},{4,6},{5,7},{6,0},{7,1},{8,10},{9,11},{10,... | collective-permute-start | bytes 196616 | tf_op jit(solution)/shard_map/ppermute | solution.py:18
  14.5 5.5 %collective-permute-start.6 = (f32[1,256,128]{2,1,0:T(8,128)S(1)}, f32[1,256,128]{2,1,0:T(8,128)S(1)}, u32[]{:S(2)}, u32[]{:S(2)}) collective-permute-start(f32[1,256,128]{2,1,0:T(8,128)S(1)} %slice.27), channel_id=1, source_target_pairs={{0,16},{8,24},{16,0},{24,8},{1,17},{9,25},{17,1},{25,9},{2,18},{10... | collective-permute-start | bytes 393224 | tf_op jit(solution)/shard_map/ppermute | solution.py:18
  17.5 7.5 %collective-permute-start.12 = (f32[256,128]{1,0:T(8,128)S(1)}, f32[256,128]{1,0:T(8,128)S(1)}, u32[]{:S(2)}, u32[]{:S(2)}) collective-permute-start(f32[256,128]{1,0:T(8,128)S(1)} %fusion.rest_2_), channel_id=1, source_target_pairs={{0,2},{1,3},{2,4},{3,5},{4,6},{5,7},{6,0},{7,1},{8,10},{9,11},{10,... | collective-permute-start | bytes 393224 | tf_op jit(solution)/shard_map/ppermute | solution.py:18
  20.0 7.2 %collective-permute-start.7 = (f32[256,128]{1,0:T(8,128)S(1)}, f32[256,128]{1,0:T(8,128)S(1)}, u32[]{:S(2)}, u32[]{:S(2)}) collective-permute-start(f32[256,128]{1,0:T(8,128)S(1)} %fusion.1.rest_2_), channel_id=1, source_target_pairs={{0,2},{1,3},{2,4},{3,5},{4,6},{5,7},{6,0},{7,1},{8,10},{9,11},{10,... | collective-permute-start | bytes 393224 | tf_op jit(solution)/shard_map/ppermute | solution.py:18
  25.1 9.1 %collective-permute-start.13 = (f32[256,128]{1,0:T(8,128)S(1)}, f32[256,128]{1,0:T(8,128)S(1)}, u32[]{:S(2)}, u32[]{:S(2)}) collective-permute-start(f32[256,128]{1,0:T(8,128)S(1)} %broadcast_select_fusion), channel_id=1, source_target_pairs={{0,1},{1,0},{2,3},{3,2},{4,5},{5,4},{6,7},{7,6},{8,9},{9,8},{10,11... | collective-permute-start | bytes 393224 | tf_op jit(solution)/shard_map/ppermute | solution.py:18
  27.2 6.6 %collective-permute-start.8 = (f32[256,128]{1,0:T(8,128)S(1)}, f32[256,128]{1,0:T(8,128)S(1)}, u32[]{:S(2)}, u32[]{:S(2)}) collective-permute-start(f32[256,128]{1,0:T(8,128)S(1)} %broadcast_select_fusion.1), channel_id=1, source_target_pairs={{0,1},{1,0},{2,3},{3,2},{4,5},{5,4},{6,7},{7,6},{8,9},{9,8},{10,11... | collective-permute-start | bytes 393224 | tf_op jit(solution)/shard_map/ppermute | solution.py:18
  30.9 5.2 %collective-permute-start.3 = (f32[128,128]{1,0:T(8,128)S(1)}, f32[128,128]{1,0:T(8,128)S(1)}, u32[]{:S(2)}, u32[]{:S(2)}) collective-permute-start(f32[128,128]{1,0:T(8,128)S(1)} %broadcast_select_fusion.2), channel_id=1, source_target_pairs={{0,1},{1,0},{2,3},{3,2},{4,5},{5,4},{6,7},{7,6},{8,9},{9,8},{10,11... | collective-permute-start | bytes 196616 | tf_op jit(solution)/shard_map/ppermute | solution.py:18
  33.8 13.6 %collective-permute-start.9 = (f32[256,128]{1,0:T(8,128)S(1)}, f32[256,128]{1,0:T(8,128)S(1)}, u32[]{:S(2)}, u32[]{:S(2)}) collective-permute-start(f32[256,128]{1,0:T(8,128)S(1)} %collective-permute-done.8.rest_2_), channel_id=1, source_target_pairs={{0,2},{1,3},{2,4},{3,5},{4,6},{5,7},{6,0},{7,1},{8,10},{9,11},{10,... | collective-permute-start | bytes 393224 | tf_op jit(solution)/shard_map/ppermute | solution.py:18
  34.1 18.1 %collective-permute-start.14 = (f32[256,128]{1,0:T(8,128)S(1)}, f32[256,128]{1,0:T(8,128)S(1)}, u32[]{:S(2)}, u32[]{:S(2)}) collective-permute-start(f32[256,128]{1,0:T(8,128)S(1)} %collective-permute-done.13.rest_2_), channel_id=1, source_target_pairs={{0,2},{1,3},{2,4},{3,5},{4,6},{5,7},{6,0},{7,1},{8,10},{9,11},{10,... | collective-permute-start | bytes 393224 | tf_op jit(solution)/shard_map/ppermute | solution.py:18
  36.1 6.8 %collective-permute-start.4 = (f32[128,128]{1,0:T(8,128)S(1)}, f32[128,128]{1,0:T(8,128)S(1)}, u32[]{:S(2)}, u32[]{:S(2)}) collective-permute-start(f32[128,128]{1,0:T(8,128)S(1)} %collective-permute-done.3.rest_2_), channel_id=1, source_target_pairs={{0,2},{1,3},{2,4},{3,5},{4,6},{5,7},{6,0},{7,1},{8,10},{9,11},{10,... | collective-permute-start | bytes 196616 | tf_op jit(solution)/shard_map/ppermute | solution.py:18
where the time goes:
time: 54.8 us; the launch traced here: 54.4 us
  Pallas kernels  21.8 us (40%)
  starting transfers between devices  19.2 us (35%)
  waiting for transfers between devices  13 us (24%)
    ppermute x15, starting transfers between devices, moved(): lax.ppermute(value, axis, [(source, target_of(source)) for source in rang...  19.2 us
    pallas_call x9, Pallas kernels, apply_part(): pl.pallas_call(functools.partial(apply_kernel, start, width, tuple(offset...  14.5 us
    ppermute x15, waiting for transfers between devices, moved(): lax.ppermute(value, axis, [(source, target_of(source)) for source in rang...  13 us
    pallas_call x1, Pallas kernels, on_device(): pl.pallas_call(functools.partial(rotate_kernel, sizes, cuts), name='rotat...  7.33 us
  transfers between devices with their start and end apart: 15, of which 7 were waited for; matrix products, arithmetic and copies ran while one was open for 0% of the time, Pallas kernels for 23%

commit v1 on v0

v1 whole, which is shorter than its diff:
```python
import functools

import jax
import jax.numpy as jnp
from jax import lax
from jax.experimental import pallas as pl
from jax.experimental.pallas import tpu as pltpu
from jax.sharding import PartitionSpec as P


F32, BF16 = jnp.float32, jnp.bfloat16
LANES, SUBLANES = 128, 8
CHUNKS = 3


def moved(value, axis, target_of):
    count = lax.axis_size(axis)
    return lax.ppermute(value, axis, [(source, target_of(source)) for source in range(count)])


def kept(array):
    return pltpu.with_memory_space_constraint(array, pltpu.HBM)


def split(value):
    high = value.astype(BF16)
    low = (value - high.astype(F32)).astype(BF16)
    return high, low


def stacked(first, second, third):
    parts = [part.astype(F32) for part in (first, second, third)]
    rows = sum(part.shape[0] for part in parts)
    fill = -rows % (2 * SUBLANES)
    if fill:
        parts.append(jnp.zeros((fill, parts[0].shape[1]), F32))
    return jnp.concatenate(parts, axis=0).astype(BF16)


def dot_first(left, right):
    return lax.dot_general(left, right, (((0,), (0,)), ((), ())), preferred_element_type=F32)


def rotate_kernel(sizes, cuts, group, *rest):
    groups, order, entries, fine, slots, val, cond, vec = sizes
    given, rest = rest[:8], rest[8:]
    outs, rest = rest[: 2 * len(cuts)], rest[2 * len(cuts) :]
    late, rest = rest[:2], rest[2:]
    held, (fine_rows, total, sems) = rest[:6], rest[6:]
    copies = [
        pltpu.make_async_copy(a, b, sems.at[i]) for i, (a, b) in enumerate(zip(given, held + late))
    ]
    for copy in copies[:6]:
        copy.start()
    src, target, slot, x_ref, val_ref, cond_ref = held
    total[...] = jnp.zeros_like(total)
    for copy in copies[:6]:
        copy.wait()
    for copy in copies[6:]:
        copy.start()
    pad = -(-val // SUBLANES) * SUBLANES
    for f in range(fine):
        x = jnp.concatenate([x_ref[f], jnp.zeros((pad - val, cond, vec), F32)], axis=0)
        high, low = split(x.reshape(pad, cond * vec))
        fine_rows[f] = stacked(high, high, low)

    def add_entry(e, carry):
        aim = target[e]

        @pl.when(aim < groups)
        def _():
            place = order(aim, group[0])
            which = slot[e]
            weights = val_ref[pl.ds(which, val, stride=slots), :]
            weights = jnp.concatenate([weights, jnp.zeros((pad - val, val), F32)], axis=0)
            weights = jnp.concatenate([weights, jnp.zeros((pad, pad - val), F32)], axis=1)
            high, low = split(weights)
            first = dot_first(stacked(high, low, high), fine_rows[src[e]])
            turned = first.reshape(pad, cond, vec)
            wide = jnp.concatenate([turned[w] for w in range(val)], axis=1)
            high, low = split(wide)
            right = stacked(high, high, low)
            high, low = split(cond_ref[which])
            second = dot_first(stacked(high, low, high), right)
            for w in range(val):
                total[place, w * cond : (w + 1) * cond, :] += second[:, w * vec : (w + 1) * vec]

        return carry

    lax.fori_loop(0, entries, add_entry, 0)
    half = groups // 2
    for i, (start, width) in enumerate(cuts):
        outs[2 * i][...] = total[0:half, start : start + width, :]
        outs[2 * i + 1][...] = total[half:groups, start : start + width, :]
    for copy in copies[6:]:
        copy.wait()


def apply_kernel(terms, has_total, blocks, *rest):
    rest = list(rest)
    out = rest.pop()
    total = rest.pop(0) if has_total else None
    energies = None if has_total else rest.pop(0)
    if has_total:
        out[...] = total[...]
    for (offset, start), ref in zip(terms, rest):
        value = ref[...]
        width, vec = value.shape
        high, low = split(value)
        block_high, block_low = split(blocks[0, offset, :, start : start + width])
        both = jnp.dot(
            block_high, jnp.concatenate([high, low], axis=1), preferred_element_type=F32
        )
        both = both[:, :vec] + both[:, vec:]
        both = both + jnp.dot(block_low, high, preferred_element_type=F32)
        if energies is not None and start == 0:
            out[...] = both
        else:
            out[...] += both
    if energies is not None:
        for (_, start), ref in zip(terms, rest):
            step = min(LANES, ref.shape[0])
            for r in range(0, ref.shape[0], step):
                rows = pl.ds(start + r, step)
                level = jnp.broadcast_to(energies[0:1, start + r : start + r + step], (step, step))
                out[rows, :] += level.T[:, 0:1] * ref[r : r + step, :]


def reversed_bits(value, bits):
    result = value * 0
    for k in range(bits):
        result = result + (((value >> k) & 1) << (bits - 1 - k))
    return result


def shifted_back(own, stops, odd):
    count = lax.axis_size("blk")
    behind = {}
    if count % 2 == 0 and stops > 2:
        behind[2] = moved(own, "blk", lambda source: (source + 2) % count)
        mixed = jnp.where(odd, behind[2], own)
        behind[1] = moved(mixed, "blk", lambda source: source ^ 1)
    elif stops > 1:
        behind[1] = moved(own, "blk", lambda source: (source + 1) % count)
    before = {0: own, **behind}
    for s in range(2, stops):
        if s not in before:
            before[s] = moved(before[s - 2], "blk", lambda source: (source + 2) % count)
            behind[s] = before[s]
    return behind


def apply_part(total, blocks, energies, terms, values):
    rows, vec = blocks.shape[2], values[0].shape[1]
    vmem = pl.BlockSpec(memory_space=pltpu.VMEM)
    return pl.pallas_call(
        functools.partial(apply_kernel, tuple(terms), total is not None),
        name="apply",
        out_shape=jax.ShapeDtypeStruct((rows, vec), F32),
        in_specs=[vmem] * (2 + len(values)),
        out_specs=vmem,
        compiler_params=pltpu.CompilerParams(vmem_limit_bytes=24 << 20),
    )(blocks, energies if total is None else total, *values)


def on_device(cuts_of, fine_coef, src, target, slot, valence, conduction, kernel, energies):
    groups = lax.axis_size("grp")
    fine, val, cond, vec = fine_coef.shape
    entries, slots = src.shape[0], valence.shape[0]
    bits = groups.bit_length() - 1
    cuts = cuts_of(val, cond)
    pairs = val * cond

    def order(aim, mine):
        return reversed_bits(aim ^ mine, bits)

    sizes = (groups, order, entries, fine, slots, val, cond, vec)
    pad = -(-val // SUBLANES) * SUBLANES
    depth = -(-3 * pad // (2 * SUBLANES)) * 2 * SUBLANES
    vmem = pl.BlockSpec(memory_space=pltpu.VMEM)
    smem = pl.BlockSpec(memory_space=pltpu.SMEM)
    hbm = pl.BlockSpec(memory_space=pltpu.HBM)
    mine, odd = lax.optimization_barrier(
        (lax.axis_index("grp").astype(jnp.int32).reshape(1), (lax.axis_index("blk") & 1) == 1)
    )
    *parts, blocks, levels = pl.pallas_call(
        functools.partial(rotate_kernel, sizes, cuts),
        name="rotate",
        out_shape=[
            jax.ShapeDtypeStruct((groups // 2, width, vec), F32) for _, width in cuts for _ in range(2)
        ]
        + [
            jax.ShapeDtypeStruct(kernel.shape, F32),
            jax.ShapeDtypeStruct(energies.shape, F32),
        ],
        in_specs=[smem] + [hbm] * 8,
        out_specs=[vmem] * (2 * len(cuts) + 2),
        scratch_shapes=[
            pltpu.SMEM((entries,), jnp.int32),
            pltpu.SMEM((entries,), jnp.int32),
            pltpu.SMEM((entries,), jnp.int32),
            pltpu.VMEM((fine, val, cond, vec), F32),
            pltpu.VMEM((val * slots, val), F32),
            pltpu.VMEM((slots, cond, cond), F32),
            pltpu.VMEM((fine, depth, cond * vec), BF16),
            pltpu.VMEM((groups, pairs, vec), F32),
            pltpu.SemaphoreType.DMA((8,)),
        ],
        compiler_params=pltpu.CompilerParams(vmem_limit_bytes=32 << 20),
    )(
        mine,
        kept(src),
        kept(target),
        kept(slot),
        kept(fine_coef),
        kept(jnp.transpose(valence, (1, 0, 2)).reshape(val * slots, val)),
        kept(conduction),
        kept(kernel),
        kept(energies),
    )

    owned, behind = [], []
    for i in range(len(cuts)):
        keep, give = parts[2 * i], parts[2 * i + 1]
        for bit in range(bits):
            got = moved(give, "grp", lambda source: source ^ (1 << bit))
            keep = keep + got
            half = keep.shape[0] // 2
            if half > 0:
                keep, give = keep[:half], keep[half:]
            else:
                keep = keep[0]
        owned.append(keep)
        behind.append(shifted_back(keep, kernel.shape[1], odd))
    starts = [start for start, _ in cuts]
    result = apply_part(None, blocks, levels, [(0, start) for start in starts], owned)
    for i, start in enumerate(starts):
        near = [s for s in behind[i] if s < 3]
        if near:
            result = apply_part(
                result, blocks, None, [(s, start) for s in near], [behind[i][s] for s in near]
            )
    for i, start in enumerate(starts):
        far = [s for s in behind[i] if s >= 3]
        if far:
            result = apply_part(
                result, blocks, None, [(s, start) for s in far], [behind[i][s] for s in far]
            )
    return result[None]


def cut_evenly(val, cond):
    step = next(w for w in range(1, val + 1) if val % w == 0 and (w * cond % LANES == 0 or w == val))
    steps = val // step
    counts = [steps * (k + 1) // CHUNKS - steps * k // CHUNKS for k in range(CHUNKS)]
    cuts, start = [], 0
    for count in counts:
        if count:
            cuts.append((start * step * cond, count * step * cond))
            start += count
    return cuts


def solution(mesh):
    spec = P(("grp", "blk"))

    def body(*args):
        return on_device(cut_evenly, *args)

    return jax.shard_map(
        body, mesh=mesh, in_specs=(spec,) * 8, out_specs=spec, check_vma=False
    )
```

time: 54.8 us -> 42.2 us (0.77)
  Pallas kernels: 21.8 us -> 9.72 us
  starting transfers between devices: 19.2 us -> 18.3 us
  waiting for transfers between devices: 13 us -> 13.7 us
    pallas_call x9 -> x7, Pallas kernels: 14.5 us -> 3.79 us  [apply_part(): pl.pallas_call(functools.partial(apply_kernel, tuple(terms), total is not...]
    pallas_call x1, Pallas kernels: 7.33 us -> 5.94 us  [on_device(): pl.pallas_call(functools.partial(rotate_kernel, sizes, cuts), name='rotat...]
    ppermute x15, starting transfers between devices: 19.2 us -> 18.3 us  [moved(): lax.ppermute(value, axis, [(source, target_of(source)) for source in rang...]
    ppermute x15, waiting for transfers between devices: 13 us -> 13.7 us  [moved(): lax.ppermute(value, axis, [(source, target_of(source)) for source in rang...]
  transfers between devices with their start and end apart: 15 -> 15, of which waited for: 7 -> 9; matrix products, arithmetic and copies ran while one was open for 0% -> 0% of each run, Pallas kernels for 23% -> 6%
where the time goes in v1:
time: 42.2 us; the launch traced here: 42 us
  starting transfers between devices  18.3 us (43%)
  waiting for transfers between devices  13.7 us (32%)
  Pallas kernels  9.72 us (23%)
    ppermute x15, starting transfers between devices, moved(): lax.ppermute(value, axis, [(source, target_of(source)) for source in rang...  18.3 us
    ppermute x15, waiting for transfers between devices, moved(): lax.ppermute(value, axis, [(source, target_of(source)) for source in rang...  13.7 us
    pallas_call x1, Pallas kernels, on_device(): pl.pallas_call(functools.partial(rotate_kernel, sizes, cuts), name='rotat...  5.94 us
    pallas_call x7, Pallas kernels, apply_part(): pl.pallas_call(functools.partial(apply_kernel, tuple(terms), total is not...  3.79 us
  transfers between devices with their start and end apart: 15, of which 9 were waited for; matrix products, arithmetic and copies ran while one was open for 0% of the time, Pallas kernels for 6%

profile of v1, /device:TPU:0, one launch (start us, length us, event | category | flops | bytes accessed | tf_op | source)
XLA Modules:
  0.0 42.0 jit_solution(17225128672672047507)
XLA Ops:
  0.0 5.9 %rotate.1 = (f32[2,128,128]{2,1,0:T(8,128)S(1)}, f32[2,128,128]{2,1,0:T(8,128)S(1)}, f32[2,256,128]{2,1,0:T(8,128)S(1)}, f32[2,256,128]{2,1,0:T(8,128)S(1)}, f32...) custom-call(s32[1]{0:T(128)} %bitcast.group, ...), custom_call_target="tpu_custom_call" | custom-call | tf_op jit(solution)/shard_map/rotate/pallas_call | solution.py:186
  6.0 0.5 %collective-permute-start = (f32[2,128,128]{2,1,0:T(8,128)S(1)}, f32[2,128,128]{2,1,0:T(8,128)S(1)}, u32[]{:S(2)}, u32[]{:S(2)}) collective-permute-start(f32[2,128,128]{2,1,0:T(8,128)S(1)} %get-tuple-element.19), channel_id=1, source_target_pairs={{0,8},{8,0},{16,24},{24,16},{1,9},{9,1},{17,25},{25,17},{2,10},{10... | collective-permute-start | bytes 393224 | tf_op jit(solution)/shard_map/ppermute | solution.py:18
  6.5 1.2 %collective-permute-done = f32[2,128,128]{2,1,0:T(8,128)S(1)} collective-permute-done((f32[2,128,128]{2,1,0:T(8,128)S(1)}, f32[2,128,128]{2,1,0:T(8,128)S(1)}, u32[]{:S(2)}, u32[]{:S(2)}) %collective-permute-start) | collective-permute-done | bytes 131104 | tf_op jit(solution)/shard_map/ppermute | solution.py:18
  7.8 2.1 %collective-permute-start.1 = (f32[1,128,128]{2,1,0:T(8,128)S(1)}, f32[1,128,128]{2,1,0:T(8,128)S(1)}, u32[]{:S(2)}, u32[]{:S(2)}) collective-permute-start(f32[1,128,128]{2,1,0:T(8,128)S(1)} %slice.25), channel_id=1, source_target_pairs={{0,16},{8,24},{16,0},{24,8},{1,17},{9,25},{17,1},{25,9},{2,18},{10... | collective-permute-start | bytes 196616 | tf_op jit(solution)/shard_map/ppermute | solution.py:18
  10.2 2.1 %collective-permute-done.1 = f32[1,128,128]{2,1,0:T(8,128)S(1)} collective-permute-done((f32[1,128,128]{2,1,0:T(8,128)S(1)}, f32[1,128,128]{2,1,0:T(8,128)S(1)}, u32[]{:S(2)}, u32[]{:S(2)}) %collective-permute-start.1) | collective-permute-done | bytes 65568 | tf_op jit(solution)/shard_map/ppermute | solution.py:18
  12.3 1.3 %collective-permute-start.6 = (f32[128,128]{1,0:T(8,128)S(1)}, f32[128,128]{1,0:T(8,128)S(1)}, u32[]{:S(2)}, u32[]{:S(2)}) collective-permute-start(f32[128,128]{1,0:T(8,128)S(1)} %fusion.2.rest_1_), channel_id=1, source_target_pairs={{0,2},{1,3},{2,4},{3,5},{4,6},{5,7},{6,0},{7,1},{8,10},{9,11},{10,... | collective-permute-start | bytes 196616 | tf_op jit(solution)/shard_map/ppermute | solution.py:18
  13.7 2.1 %collective-permute-start.5 = (f32[1,256,128]{2,1,0:T(8,128)S(1)}, f32[1,256,128]{2,1,0:T(8,128)S(1)}, u32[]{:S(2)}, u32[]{:S(2)}) collective-permute-start(f32[1,256,128]{2,1,0:T(8,128)S(1)} %slice.29), channel_id=1, source_target_pairs={{0,16},{8,24},{16,0},{24,8},{1,17},{9,25},{17,1},{25,9},{2,18},{10... | collective-permute-start | bytes 393224 | tf_op jit(solution)/shard_map/ppermute | solution.py:18
  15.7 0.6 %collective-permute-done.3 = f32[1,256,128]{2,1,0:T(8,128)S(1)} collective-permute-done((f32[1,256,128]{2,1,0:T(8,128)S(1)}, f32[1,256,128]{2,1,0:T(8,128)S(1)}, u32[]{:S(2)}, u32[]{:S(2)}) %collective-permute-start.3) | collective-permute-done | bytes 131104 | tf_op jit(solution)/shard_map/ppermute | solution.py:18
  16.4 2.3 %collective-permute-start.8 = (f32[256,128]{1,0:T(8,128)S(1)}, f32[256,128]{1,0:T(8,128)S(1)}, u32[]{:S(2)}, u32[]{:S(2)}) collective-permute-start(f32[256,128]{1,0:T(8,128)S(1)} %fusion.1.rest_2_), channel_id=1, source_target_pairs={{0,2},{1,3},{2,4},{3,5},{4,6},{5,7},{6,0},{7,1},{8,10},{9,11},{10,... | collective-permute-start | bytes 393224 | tf_op jit(solution)/shard_map/ppermute | solution.py:18
  18.7 2.9 %collective-permute-start.10 = (f32[256,128]{1,0:T(8,128)S(1)}, f32[256,128]{1,0:T(8,128)S(1)}, u32[]{:S(2)}, u32[]{:S(2)}) collective-permute-start(f32[256,128]{1,0:T(8,128)S(1)} %fusion.rest_3_), channel_id=1, source_target_pairs={{0,2},{1,3},{2,4},{3,5},{4,6},{5,7},{6,0},{7,1},{8,10},{9,11},{10,... | collective-permute-start | bytes 393224 | tf_op jit(solution)/shard_map/ppermute | solution.py:18
  21.6 2.3 %collective-permute-done.8.rest_1_ = f32[256,128]{1,0:T(8,128)S(1)} collective-permute-done((f32[256,128]{1,0:T(8,128)S(1)}, f32[256,128]{1,0:T(8,128)S(1)}, u32[]{:S(2)}, u32[]{:S(2)}) %collective-permute-start.8) | collective-permute-done | bytes 131104 | tf_op jit(solution)/shard_map/ppermute | solution.py:18
  24.0 0.8 %collective-permute-start.9 = (f32[256,128]{1,0:T(8,128)S(1)}, f32[256,128]{1,0:T(8,128)S(1)}, u32[]{:S(2)}, u32[]{:S(2)}) collective-permute-start(f32[256,128]{1,0:T(8,128)S(1)} %broadcast_select_fusion.1), channel_id=1, source_target_pairs={{0,1},{1,0},{2,3},{3,2},{4,5},{5,4},{6,7},{7,6},{8,9},{9,8},{10,11... | collective-permute-start | bytes 393224 | tf_op jit(solution)/shard_map/ppermute | solution.py:18
  24.8 1.2 %collective-permute-done.10.rest_1_ = f32[256,128]{1,0:T(8,128)S(1)} collective-permute-done((f32[256,128]{1,0:T(8,128)S(1)}, f32[256,128]{1,0:T(8,128)S(1)}, u32[]{:S(2)}, u32[]{:S(2)}) %collective-permute-start.10) | collective-permute-done | bytes 131104 | tf_op jit(solution)/shard_map/ppermute | solution.py:18
  26.0 3.5 %collective-permute-start.11 = (f32[256,128]{1,0:T(8,128)S(1)}, f32[256,128]{1,0:T(8,128)S(1)}, u32[]{:S(2)}, u32[]{:S(2)}) collective-permute-start(f32[256,128]{1,0:T(8,128)S(1)} %broadcast_select_fusion), channel_id=1, source_target_pairs={{0,1},{1,0},{2,3},{3,2},{4,5},{5,4},{6,7},{7,6},{8,9},{9,8},{10,11... | collective-permute-start | bytes 393224 | tf_op jit(solution)/shard_map/ppermute | solution.py:18
  29.6 0.6 %collective-permute-done.9.rest_2_ = f32[256,128]{1,0:T(8,128)S(1)} collective-permute-done((f32[256,128]{1,0:T(8,128)S(1)}, f32[256,128]{1,0:T(8,128)S(1)}, u32[]{:S(2)}, u32[]{:S(2)}) %collective-permute-start.9) | collective-permute-done | bytes 131104 | tf_op jit(solution)/shard_map/ppermute | solution.py:18
  30.2 1.2 %collective-permute-start.13 = (f32[256,128]{1,0:T(8,128)S(1)}, f32[256,128]{1,0:T(8,128)S(1)}, u32[]{:S(2)}, u32[]{:S(2)}) collective-permute-start(f32[256,128]{1,0:T(8,128)S(1)} %collective-permute-done.9.rest_2_), channel_id=1, source_target_pairs={{0,2},{1,3},{2,4},{3,5},{4,6},{5,7},{6,0},{7,1},{8,10},{9,11},{10,... | collective-permute-start | bytes 393224 | tf_op jit(solution)/shard_map/ppermute | solution.py:18
  31.3 1.2 %collective-permute-done.11.rest_2_ = f32[256,128]{1,0:T(8,128)S(1)} collective-permute-done((f32[256,128]{1,0:T(8,128)S(1)}, f32[256,128]{1,0:T(8,128)S(1)}, u32[]{:S(2)}, u32[]{:S(2)}) %collective-permute-start.11) | collective-permute-done | bytes 131104 | tf_op jit(solution)/shard_map/ppermute | solution.py:18
  32.7 1.1 %collective-permute-done.7.rest_2_ = f32[128,128]{1,0:T(8,128)S(1)} collective-permute-done((f32[128,128]{1,0:T(8,128)S(1)}, f32[128,128]{1,0:T(8,128)S(1)}, u32[]{:S(2)}, u32[]{:S(2)}) %collective-permute-start.7) | collective-permute-done | bytes 65568 | tf_op jit(solution)/shard_map/ppermute | solution.py:18
  33.8 1.0 %collective-permute-start.12 = (f32[128,128]{1,0:T(8,128)S(1)}, f32[128,128]{1,0:T(8,128)S(1)}, u32[]{:S(2)}, u32[]{:S(2)}) collective-permute-start(f32[128,128]{1,0:T(8,128)S(1)} %collective-permute-done.7.rest_2_), channel_id=1, source_target_pairs={{0,2},{1,3},{2,4},{3,5},{4,6},{5,7},{6,0},{7,1},{8,10},{9,11},{10,... | collective-permute-start | bytes 196616 | tf_op jit(solution)/shard_map/ppermute | solution.py:18
  34.8 0.6 %apply.7.rest_0_ = f32[640,128]{1,0:T(8,128)S(1)} custom-call(f32[1,4,640,640]{3,2,1,0:T(8,128)S(1)} %get-tuple-element.16.blocks, f32[1,640]{1,0:T(1,128)S(1)} %get-tuple-element.17.rest_0_, f32[128,128]{1,0:T(8,128)S(1)} %fusion.2.rest_1_, f32[256,128]{1,0:T(8,128)S(1)} %fusion.1.rest_2_, f32[256,128]{1,0:T(8,128)S(1)} %fusion.rest_3_), custom_call_target="tpu_custom_call" | custom-call | tf_op jit(solution)/shard_map/apply/pallas_call | solution.py:156
  35.8 0.5 %apply.9.rest_0_ = f32[640,128]{1,0:T(8,128)S(1)} custom-call(f32[1,4,640,640]{3,2,1,0:T(8,128)S(1)} %get-tuple-element.16.blocks, f32[640,128]{1,0:T(8,128)S(1)} %apply.8.rest_0_, f32[256,128]{1,0:T(8,128)S(1)} %collective-permute-done.8.rest_1_, f32[256,128]{1,0:T(8,128)S(1)} %collective-permute-done.9.rest_2_), custom_call_target="tpu_custom_call" | custom-call | tf_op jit(solution)/shard_map/apply/pallas_call | solution.py:156
  36.3 0.5 %apply.10.rest_0_ = f32[640,128]{1,0:T(8,128)S(1)} custom-call(f32[1,4,640,640]{3,2,1,0:T(8,128)S(1)} %get-tuple-element.16.blocks, f32[640,128]{1,0:T(8,128)S(1)} %apply.9.rest_0_, f32[256,128]{1,0:T(8,128)S(1)} %collective-permute-done.10.rest_1_, f32[256,128]{1,0:T(8,128)S(1)} %collective-permute-done.11.rest_2_), custom_call_target="tpu_custom_call" | custom-call | tf_op jit(solution)/shard_map/apply/pallas_call | solution.py:156
  36.9 3.4 %collective-permute-done.12.rest_1_ = f32[128,128]{1,0:T(8,128)S(1)} collective-permute-done((f32[128,128]{1,0:T(8,128)S(1)}, f32[128,128]{1,0:T(8,128)S(1)}, u32[]{:S(2)}, u32[]{:S(2)}) %collective-permute-start.12) | collective-permute-done | bytes 65568 | tf_op jit(solution)/shard_map/ppermute | solution.py:18
  40.9 1.1 %apply.13 = f32[640,128]{1,0:T(8,128)} custom-call(f32[1,4,640,640]{3,2,1,0:T(8,128)S(1)} %get-tuple-element.16.blocks, f32[640,128]{1,0:T(8,128)S(1)} %apply.12.rest_0_, f32[256,128]{1,0:T(8,128)S(1)} %collective-permute-done.14.rest_1_), custom_call_target="tpu_custom_call" | custom-call | tf_op jit(solution)/shard_map/apply/pallas_call | solution.py:156
  (26 shorter events, 1.9 us)
Async XLA Ops:
  5.9 3.9 %collective-permute-start.2 = (f32[2,256,128]{2,1,0:T(8,128)S(1)}, f32[2,256,128]{2,1,0:T(8,128)S(1)}, u32[]{:S(2)}, u32[]{:S(2)}) collective-permute-start(f32[2,256,128]{2,1,0:T(8,128)S(1)} %get-tuple-element.21), channel_id=1, source_target_pairs={{0,8},{8,0},{16,24},{24,16},{1,9},{9,1},{17,25},{25,17},{2,10},{10... | collective-permute-start | bytes 786440 | tf_op jit(solution)/shard_map/ppermute | solution.py:18
  6.0 1.7 %collective-permute-start = (f32[2,128,128]{2,1,0:T(8,128)S(1)}, f32[2,128,128]{2,1,0:T(8,128)S(1)}, u32[]{:S(2)}, u32[]{:S(2)}) collective-permute-start(f32[2,128,128]{2,1,0:T(8,128)S(1)} %get-tuple-element.19), channel_id=1, source_target_pairs={{0,8},{8,0},{16,24},{24,16},{1,9},{9,1},{17,25},{25,17},{2,10},{10... | collective-permute-start | bytes 393224 | tf_op jit(solution)/shard_map/ppermute | solution.py:18
  7.8 4.6 %collective-permute-start.1 = (f32[1,128,128]{2,1,0:T(8,128)S(1)}, f32[1,128,128]{2,1,0:T(8,128)S(1)}, u32[]{:S(2)}, u32[]{:S(2)}) collective-permute-start(f32[1,128,128]{2,1,0:T(8,128)S(1)} %slice.25), channel_id=1, source_target_pairs={{0,16},{8,24},{16,0},{24,8},{1,17},{9,25},{17,1},{25,9},{2,18},{10... | collective-permute-start | bytes 196616 | tf_op jit(solution)/shard_map/ppermute | solution.py:18
  9.8 3.8 %collective-permute-start.4 = (f32[2,256,128]{2,1,0:T(8,128)S(1)}, f32[2,256,128]{2,1,0:T(8,128)S(1)}, u32[]{:S(2)}, u32[]{:S(2)}) collective-permute-start(f32[2,256,128]{2,1,0:T(8,128)S(1)} %get-tuple-element.23), channel_id=1, source_target_pairs={{0,8},{8,0},{16,24},{24,16},{1,9},{9,1},{17,25},{25,17},{2,10},{10... | collective-permute-start | bytes 786440 | tf_op jit(solution)/shard_map/ppermute | solution.py:18
  9.9 6.4 %collective-permute-start.3 = (f32[1,256,128]{2,1,0:T(8,128)S(1)}, f32[1,256,128]{2,1,0:T(8,128)S(1)}, u32[]{:S(2)}, u32[]{:S(2)}) collective-permute-start(f32[1,256,128]{2,1,0:T(8,128)S(1)} %slice.27), channel_id=1, source_target_pairs={{0,16},{8,24},{16,0},{24,8},{1,17},{9,25},{17,1},{25,9},{2,18},{10... | collective-permute-start | bytes 393224 | tf_op jit(solution)/shard_map/ppermute | solution.py:18
  12.3 17.1 %collective-permute-start.6 = (f32[128,128]{1,0:T(8,128)S(1)}, f32[128,128]{1,0:T(8,128)S(1)}, u32[]{:S(2)}, u32[]{:S(2)}) collective-permute-start(f32[128,128]{1,0:T(8,128)S(1)} %fusion.2.rest_1_), channel_id=1, source_target_pairs={{0,2},{1,3},{2,4},{3,5},{4,6},{5,7},{6,0},{7,1},{8,10},{9,11},{10,... | collective-permute-start | bytes 196616 | tf_op jit(solution)/shard_map/ppermute | solution.py:18
  13.7 5.0 %collective-permute-start.5 = (f32[1,256,128]{2,1,0:T(8,128)S(1)}, f32[1,256,128]{2,1,0:T(8,128)S(1)}, u32[]{:S(2)}, u32[]{:S(2)}) collective-permute-start(f32[1,256,128]{2,1,0:T(8,128)S(1)} %slice.29), channel_id=1, source_target_pairs={{0,16},{8,24},{16,0},{24,8},{1,17},{9,25},{17,1},{25,9},{2,18},{10... | collective-permute-start | bytes 393224 | tf_op jit(solution)/shard_map/ppermute | solution.py:18
  16.4 7.6 %collective-permute-start.8 = (f32[256,128]{1,0:T(8,128)S(1)}, f32[256,128]{1,0:T(8,128)S(1)}, u32[]{:S(2)}, u32[]{:S(2)}) collective-permute-start(f32[256,128]{1,0:T(8,128)S(1)} %fusion.1.rest_2_), channel_id=1, source_target_pairs={{0,2},{1,3},{2,4},{3,5},{4,6},{5,7},{6,0},{7,1},{8,10},{9,11},{10,... | collective-permute-start | bytes 393224 | tf_op jit(solution)/shard_map/ppermute | solution.py:18
  18.7 7.3 %collective-permute-start.10 = (f32[256,128]{1,0:T(8,128)S(1)}, f32[256,128]{1,0:T(8,128)S(1)}, u32[]{:S(2)}, u32[]{:S(2)}) collective-permute-start(f32[256,128]{1,0:T(8,128)S(1)} %fusion.rest_3_), channel_id=1, source_target_pairs={{0,2},{1,3},{2,4},{3,5},{4,6},{5,7},{6,0},{7,1},{8,10},{9,11},{10,... | collective-permute-start | bytes 393224 | tf_op jit(solution)/shard_map/ppermute | solution.py:18
  24.0 6.2 %collective-permute-start.9 = (f32[256,128]{1,0:T(8,128)S(1)}, f32[256,128]{1,0:T(8,128)S(1)}, u32[]{:S(2)}, u32[]{:S(2)}) collective-permute-start(f32[256,128]{1,0:T(8,128)S(1)} %broadcast_select_fusion.1), channel_id=1, source_target_pairs={{0,1},{1,0},{2,3},{3,2},{4,5},{5,4},{6,7},{7,6},{8,9},{9,8},{10,11... | collective-permute-start | bytes 393224 | tf_op jit(solution)/shard_map/ppermute | solution.py:18
  26.0 6.5 %collective-permute-start.11 = (f32[256,128]{1,0:T(8,128)S(1)}, f32[256,128]{1,0:T(8,128)S(1)}, u32[]{:S(2)}, u32[]{:S(2)}) collective-permute-start(f32[256,128]{1,0:T(8,128)S(1)} %broadcast_select_fusion), channel_id=1, source_target_pairs={{0,1},{1,0},{2,3},{3,2},{4,5},{5,4},{6,7},{7,6},{8,9},{9,8},{10,11... | collective-permute-start | bytes 393224 | tf_op jit(solution)/shard_map/ppermute | solution.py:18
  29.5 4.3 %collective-permute-start.7 = (f32[128,128]{1,0:T(8,128)S(1)}, f32[128,128]{1,0:T(8,128)S(1)}, u32[]{:S(2)}, u32[]{:S(2)}) collective-permute-start(f32[128,128]{1,0:T(8,128)S(1)} %broadcast_select_fusion.2), channel_id=1, source_target_pairs={{0,1},{1,0},{2,3},{3,2},{4,5},{5,4},{6,7},{7,6},{8,9},{9,8},{10,11... | collective-permute-start | bytes 196616 | tf_op jit(solution)/shard_map/ppermute | solution.py:18
  30.2 10.4 %collective-permute-start.13 = (f32[256,128]{1,0:T(8,128)S(1)}, f32[256,128]{1,0:T(8,128)S(1)}, u32[]{:S(2)}, u32[]{:S(2)}) collective-permute-start(f32[256,128]{1,0:T(8,128)S(1)} %collective-permute-done.9.rest_2_), channel_id=1, source_target_pairs={{0,2},{1,3},{2,4},{3,5},{4,6},{5,7},{6,0},{7,1},{8,10},{9,11},{10,... | collective-permute-start | bytes 393224 | tf_op jit(solution)/shard_map/ppermute | solution.py:18
  32.5 8.4 %collective-permute-start.14 = (f32[256,128]{1,0:T(8,128)S(1)}, f32[256,128]{1,0:T(8,128)S(1)}, u32[]{:S(2)}, u32[]{:S(2)}) collective-permute-start(f32[256,128]{1,0:T(8,128)S(1)} %collective-permute-done.11.rest_2_), channel_id=1, source_target_pairs={{0,2},{1,3},{2,4},{3,5},{4,6},{5,7},{6,0},{7,1},{8,10},{9,11},{10,... | collective-permute-start | bytes 393224 | tf_op jit(solution)/shard_map/ppermute | solution.py:18
  33.8 6.5 %collective-permute-start.12 = (f32[128,128]{1,0:T(8,128)S(1)}, f32[128,128]{1,0:T(8,128)S(1)}, u32[]{:S(2)}, u32[]{:S(2)}) collective-permute-start(f32[128,128]{1,0:T(8,128)S(1)} %collective-permute-done.7.rest_2_), channel_id=1, source_target_pairs={{0,2},{1,3},{2,4},{3,5},{4,6},{5,7},{6,0},{7,1},{8,10},{9,11},{10,... | collective-permute-start | bytes 196616 | tf_op jit(solution)/shard_map/ppermute | solution.py:18
